TPU v7x, 128 devices: a whole 4x4x4 slice. The times are simulated.
128 devices in a mesh: sec: 2 (over y_lo), dp: 16 (over z, y_hi, core), tensor: 4 (over x).
Axes of the slice: x: 4, y: 4 (y_hi: 2, y_lo: 2; y = y_hi * 2 + y_lo), z: 4, core: 2. Of those that a mesh axis runs over, the one named last changes fastest.
Arguments:
- student_rows: bfloat16 [2, 8192, 5376], P('sec', 'dp'), may hold values from -24 to 24
- teacher_rows: bfloat16 [2, 8192, 5376], P('sec', 'dp'), may hold values from -6 to 6
- norm_gain: float32 [5376], replicated, may hold values from 0.5 to 1.5
- post_gain: float32 [5376], replicated, may hold values from 0.5 to 1.5
- query_weight: bfloat16 [5376, 2048], P(('sec', 'dp'), 'tensor')
- key_weight: bfloat16 [5376, 1024], P(('sec', 'dp'), 'tensor')
- value_weight: bfloat16 [5376, 1024], P(('sec', 'dp'), 'tensor'), may hold values from -0.078125 to 0.078125
- out_weight: bfloat16 [5376, 2048], P(('sec', 'dp'), 'tensor'), may hold values from -0.125 to 0.125
Outputs:
- layer_output: bfloat16 [2, 8192, 5376], P('sec', 'dp', 'tensor')
- query_grad: float32 [5376, 2048], P(('sec', 'dp'), 'tensor')
- output_grad: float32 [5376, 2048], P(('sec', 'dp'), 'tensor')
All inputs are finite; a program needn't handle non-finite values.
Results may differ from a plain program's by a relative error of at most 0.025.
The roundings to bfloat16 on the way count: a program that leaves them out, or rounds other values in their place, can miss the bound.
Values may be sent and summed in bfloat16 or wider, within the bound.
A program may use at most 128 MiB of HBM per device.

v0:
```python
import math

import jax
import jax.numpy as jnp
from jax import lax
from jax.sharding import PartitionSpec as P

HEADS = 8
KV_HEADS = 4
HD = 256
W = 1024


norm_eps = 1e-06
rope_base = 10000.0
masked_score = -1e30


def from_partner(block, axis, bit):
    count = lax.axis_size(axis)
    route = []
    for low in range(count):
        high = low | 1 << bit
        if high != low and high < count:
            route += [(low, high), (high, low)]
    return lax.ppermute(block, axis, route)


def from_behind(x, axis, by):
    count = lax.axis_size(axis)
    pairs = [(i, i + by) for i in range(count) if 0 <= i + by < count]
    return lax.ppermute(x, axis, pairs)


def rotate(values, cos_table, sin_table, sign_value):
    row_count = values.shape[0]
    half_dim = cos_table.shape[1]
    per_head = values.reshape(row_count, -1, 2 * half_dim)
    leading = per_head[:, :, :half_dim]
    trailing = per_head[:, :, half_dim:]
    cosines = cos_table[:, None, :]
    sin_scaled = sign_value * sin_table[:, None, :]
    rotated = jnp.concatenate(
        [leading * cosines - trailing * sin_scaled, trailing * cosines + leading * sin_scaled],
        axis=2,
    )
    return rotated.reshape(row_count, -1)


def shards(
    student_rows,
    teacher_rows,
    norm_gain,
    post_gain,
    query_weight,
    key_weight,
    value_weight,
    out_weight,
):
    tok_count = student_rows.shape[1]
    model_width = student_rows.shape[2]
    tensor_count = lax.axis_size("tensor")
    share_cols = model_width // tensor_count
    data_count = lax.axis_size("sec") * lax.axis_size("dp")
    blocks_back = (W + tok_count - 1) // tok_count
    key_count = (blocks_back + 1) * tok_count
    local_groups = key_weight.shape[1] // HD
    group_size = HEADS // KV_HEADS
    query_cols = query_weight.shape[1]
    score_scale = 1.0 / math.sqrt(HD)
    loss_scale = 2.0 / math.sqrt(data_count * tok_count)
    target = from_partner(teacher_rows[0], "sec", 0)
    query_full, key_full, value_full, out_full = (
        lax.all_gather(query_weight, ("sec", "dp"), axis=0, tiled=True),
        lax.all_gather(key_weight, ("sec", "dp"), axis=0, tiled=True),
        lax.all_gather(value_weight, ("sec", "dp"), axis=0, tiled=True),
        lax.all_gather(out_weight, ("sec", "dp"), axis=0, tiled=True),
    )
    student_f = student_rows[0].astype(jnp.float32)
    inverse = lax.rsqrt(jnp.mean(student_f * student_f, axis=1, keepdims=True) + norm_eps)
    normed = (student_f * inverse * norm_gain).astype(jnp.bfloat16)
    first_pos = lax.axis_index("dp") * tok_count
    half_dim = HD // 2
    inv_freq = jnp.power(
        jnp.float32(rope_base), -2.0 * jnp.arange(half_dim, dtype=jnp.float32) / HD
    )
    positions = (first_pos + jnp.arange(tok_count, dtype=jnp.int32)).astype(jnp.float32)
    angles = positions[:, None] * inv_freq[None, :]
    cos_table = jnp.cos(angles)
    sin_table = jnp.sin(angles)
    queries = rotate(
        jnp.dot(normed, query_full, preferred_element_type=jnp.float32), cos_table, sin_table, 1.0
    ).astype(jnp.bfloat16)
    key_rows = rotate(
        jnp.dot(normed, key_full, preferred_element_type=jnp.float32), cos_table, sin_table, 1.0
    ).astype(jnp.bfloat16)
    value_rows = jnp.dot(normed, value_full, preferred_element_type=jnp.float32).astype(
        jnp.bfloat16
    )
    key_parts = [key_rows]
    value_parts = [value_rows]
    for offset in range(1, blocks_back + 1):
        earlier_keys, earlier_values = from_behind((key_rows, value_rows), "dp", offset)
        key_parts = [earlier_keys] + key_parts
        value_parts = [earlier_values] + value_parts
    key_window = jnp.concatenate(key_parts, axis=0)
    value_window = jnp.concatenate(value_parts, axis=0)
    query_pos = first_pos + jnp.arange(tok_count, dtype=jnp.int32)
    key_pos = first_pos - blocks_back * tok_count + jnp.arange(key_count, dtype=jnp.int32)
    allowed = (
        (key_pos[None, :] >= 0)
        & (key_pos[None, :] <= query_pos[:, None])
        & (key_pos[None, :] > query_pos[:, None] - W)
    )
    grouped_q = queries.reshape(tok_count, local_groups, group_size, HD)
    grouped_k = key_window.reshape(key_count, local_groups, HD)
    grouped_v = value_window.reshape(key_count, local_groups, HD)
    scores = (
        jnp.einsum("tgad,kgd->gatk", grouped_q, grouped_k, preferred_element_type=jnp.float32)
        * score_scale
    )
    scores = jnp.where(allowed, scores, masked_score)
    row_peak = jnp.max(scores, axis=3, keepdims=True)
    exp_scores = jnp.exp(scores - row_peak)
    attn_probs = exp_scores / jnp.sum(exp_scores, axis=3, keepdims=True)
    probs_b = attn_probs.astype(jnp.bfloat16)
    mixed_rows = (
        jnp.einsum("gatk,kgd->tgad", probs_b, grouped_v, preferred_element_type=jnp.float32)
        .astype(jnp.bfloat16)
        .reshape(tok_count, query_cols)
    )
    partial_value = jnp.einsum(
        "te,de->td", mixed_rows, out_full, preferred_element_type=jnp.float32
    )
    summed = lax.psum(partial_value.astype(jnp.bfloat16), "tensor").astype(jnp.float32)
    post_factor = lax.rsqrt(jnp.mean(summed * summed, axis=1, keepdims=True) + norm_eps)
    layer_full = (student_f + summed * post_factor * post_gain).astype(jnp.bfloat16)
    loss_grad = loss_scale * (layer_full.astype(jnp.float32) - target.astype(jnp.float32))
    scaled = post_gain * loss_grad
    along_sum = jnp.mean(summed * scaled, axis=1, keepdims=True)
    pre_grad = (
        post_factor * scaled - summed * post_factor * post_factor * post_factor * along_sum
    ).astype(jnp.bfloat16)
    mixed_grad = jnp.dot(pre_grad, out_full, preferred_element_type=jnp.float32).astype(
        jnp.bfloat16
    )
    grouped_g = mixed_grad.reshape(tok_count, local_groups, group_size, HD)
    prob_grad = jnp.einsum(
        "tgad,kgd->gatk", grouped_g, grouped_v, preferred_element_type=jnp.float32
    )
    score_grad = (
        attn_probs * (prob_grad - jnp.sum(attn_probs * prob_grad, axis=3, keepdims=True))
    ).astype(jnp.bfloat16)
    rotated_grad = (
        jnp.einsum(
            "gatk,kgd->tgad", score_grad, grouped_k, preferred_element_type=jnp.float32
        ).reshape(tok_count, query_cols)
        * score_scale
    )
    query_pre = rotate(rotated_grad, cos_table, sin_table, -1.0).astype(jnp.bfloat16)
    query_term = jnp.einsum("td,te->de", normed, query_pre, preferred_element_type=jnp.float32)
    out_term = jnp.einsum("td,te->de", pre_grad, mixed_rows, preferred_element_type=jnp.float32)
    grad_owned = lax.psum_scatter(
        jnp.concatenate([query_term, out_term], axis=1).astype(jnp.bfloat16),
        ("sec", "dp"),
        scatter_dimension=0,
        tiled=True,
    ).astype(jnp.float32)
    layer_share = lax.dynamic_slice_in_dim(
        layer_full, lax.axis_index("tensor") * share_cols, share_cols, 1
    )
    return (layer_share[None], grad_owned[:, :query_cols], grad_owned[:, query_cols:])


def solution(mesh):
    in_specs = (
        P("sec", "dp", None),
        P("sec", "dp", None),
        P(),
        P(),
        P(("sec", "dp"), "tensor"),
        P(("sec", "dp"), "tensor"),
        P(("sec", "dp"), "tensor"),
        P(("sec", "dp"), "tensor"),
    )
    out_specs = (P("sec", "dp", "tensor"), P(("sec", "dp"), "tensor"), P(("sec", "dp"), "tensor"))
    return jax.shard_map(shards, mesh=mesh, in_specs=in_specs, out_specs=out_specs, check_vma=False)
```

profile of v0, /device:TPU:7, one launch (start us, length us, event | category | flops | bytes accessed | tf_op | source)
XLA Modules:
  0.0 622.8 jit_solution(17924069632204809534)
XLA Ops:
  10.1 3.7 fusion.9
  16.0 54.0 %all-gather.7.cloned.1.call-done = bf16[5376,256]{1,0:T(8,128)(2,1)} async-done(((bf16[168,256]{1,0:T(8,128)(2,1)}), bf16[5376,256]{1,0:T(8,128)(2,1)}) %all-gather.7.cloned.1.call-update) | async-done | bytes 2752528 | tf_op jit(solution)/shard_map/all_gather | solution.py:75
  70.0 5.4 fusion.50
  76.6 3.9 collective-permute-start.3
  80.5 3.8 collective-permute-start.2
  84.3 51.6 %all-gather.5.cloned.1.call-done = bf16[5376,256]{1,0:T(8,128)(2,1)} async-done(((bf16[168,256]{1,0:T(8,128)(2,1)}), bf16[5376,256]{1,0:T(8,128)(2,1)}) %all-gather.5.cloned.1.call-update) | async-done | bytes 2752528 | tf_op jit(solution)/shard_map/all_gather | solution.py:76
  136.0 5.1 fusion.53
  141.0 3.8 collective-permute-start.1
  148.1 56.7 %all-gather.9.cloned.1.call-done = bf16[5376,512]{1,0:T(8,128)(2,1)} async-done(((bf16[168,512]{1,0:T(8,128)(2,1)}), bf16[5376,512]{1,0:T(8,128)(2,1)}) %all-gather.9.cloned.1.call-update) | async-done | bytes 5505040 | tf_op jit(solution)/shard_map/all_gather | solution.py:74
  204.8 8.3 %copy.30 = bf16[512,5376]{1,0:T(8,128)(2,1)} copy(bf16[512,5376]{0,1:T(8,128)(2,1)} %bitcast.134) | data formatting | bytes 11010048 | tf_op jit(solution)/shard_map/dot_general | solution.py:92
  213.1 7.0 %fusion.22 = f32[512,2,256]{0,2,1:T(8,128)S(1)} fusion(bf16[2,256,5376]{2,1,0:T(8,128)(2,1)} %bitcast.135, bf16[1,512,5376]{2,1,0:T(8,128)(2,1)} %param.8, f32[5376]{0:T(1024)S(1)} %copy-done.4, f32[512]{0:T(512)S(1)} %add_rsqrt_fusion.1), kind=kOutput, calls=%fused_computation.36 | convolution fusion | flops 2829582336 | bytes 12082176 | tf_op jit(solution)/shard_map/dot_general | solution.py:92
  227.4 39.8 %all-gather.11.cloned.1.call-done = bf16[5376,512]{1,0:T(8,128)(2,1)} async-done(((bf16[168,512]{1,0:T(8,128)(2,1)}), bf16[5376,512]{1,0:T(8,128)(2,1)}) %all-gather.11.cloned.1.call-update) | async-done | bytes 5505040 | tf_op jit(solution)/shard_map/all_gather | solution.py:77
  267.2 8.3 %convolution_convert_fusion.2 = bf16[512,5376]{1,0:T(8,128)(2,1)} fusion(bf16[512,512]{0,1:T(8,128)(2,1)} %bitcast.139, bf16[5376,512]{1,0:T(8,128)(2,1)} %all-gather.11.cloned.1.call-done), kind=kOutput, calls=%fused_computation.26 | convolution fusion | flops 2821324800 | bytes 11534336 | tf_op jit(solution)/shard_map/te,de->td/dot_general | solution.py:132
  276.7 109.8 %all-reduce.2.cloned.1.call-done = bf16[512,5376]{1,0:T(8,128)(2,1)} async-done(((bf16[512,5376]{1,0:T(8,128)(2,1)}), bf16[512,5376]{1,0:T(8,128)(2,1)}) %all-reduce.2.cloned.1.call-update) | async-done | bytes 5505040 | tf_op jit(solution)/shard_map/psum | solution.py:135
  386.5 3.9 fusion.15
  390.4 5.7 collective-permute-done.4
  396.1 7.1 %fusion.16 = (f32[512]{0:T(512)S(1)}, bf16[512,5376]{1,0:T(8,128)(2,1)S(1)}) fusion(bf16[512,5376]{1,0:T(8,128)(2,1)S(1)} %copy-done, bf16[512,5376]{1,0:T(8,128)(2,1)} %collective-permute-done.4, f32[5376]{0:T(1024)S(1)} %broadcast_multiply_fusion.1, f32[5376]{0:T(1024)S(1)} %copy-done.3, f32[512]{0:T(512)S(1)} %add_rsqrt_fusion, bf16[1,512,5376]{2,1,0:T(8,128)(2,1)} %param.8), kind=kLoop, calls=%fused_computation.21 | loop fusion | flops 33029632 | bytes 22067200 | tf_op jit(solution)/shard_map/reduce_sum | solution.py:140
  403.2 8.0 %fusion.8 = bf16[512,5376]{1,0:T(8,128)(2,1)S(1)} fusion(bf16[512,5376]{1,0:T(8,128)(2,1)S(1)} %copy-done, bf16[512,5376]{1,0:T(8,128)(2,1)} %collective-permute-done.4, bf16[512,5376]{1,0:T(8,128)(2,1)S(1)} %get-tuple-element.13, f32[512]{0:T(512)S(1)} %broadcast_multiply_fusion.2, f32[5376]{0:T(1024)S(1)} %broadcast_multiply_fusion.1, f32[512]{0:T(512)S(1)} %add_rsqrt_fusion), kind=kLoop, calls=%fused_computation.13 | loop fusion | flops 33030144 | bytes 22045696 | tf_op jit(solution)/shard_map/convert_element_type | solution.py:143
  411.2 3.2 convolution_convert_fusion
  414.4 5.8 convolution_convert_fusion.3
  425.6 3.6 convolution_convert_fusion.1
  429.2 5.1 pad_maximum_fusion
  434.3 14.7 %copy.48 = bf16[5376,1024]{1,0:T(8,128)(2,1)} copy(bf16[5376,1024]{0,1:T(8,128)(2,1)} %pad_maximum_fusion) | data formatting | bytes 22020096
  452.8 159.6 %reduce-scatter.4.cloned.1.call-done = bf16[168,1024]{1,0:T(8,128)(2,1)} async-done(((bf16[5376,1024]{1,0:T(8,128)(2,1)}), bf16[168,1024]{1,0:T(8,128)(2,1)}) %reduce-scatter.4.cloned.1.call-update) | async-done | bytes 344080
  (67 shorter events, 30.2 us)
Async XLA Ops:
  7.2 62.9 %copy-start.4 = (f32[5376]{0:T(1024)S(1)}, f32[5376]{0:T(1024)}, u32[]{:S(2)}) copy-start(f32[5376]{0:T(1024)} %param.10) | copy-start | bytes 64516
  7.2 62.9 %all-gather.7.cloned.1.call-start = ((), (), s32[]{:S(2)}) async-start(), calls=%async_computation.2 | async-start | bytes 2838528 | tf_op jit(solution)/shard_map/all_gather | solution.py:75
  7.9 128.1 %all-gather.5.cloned.1.call-start = ((), (), s32[]{:S(2)}) async-start(), calls=%async_computation.1 | async-start | bytes 2838528 | tf_op jit(solution)/shard_map/all_gather | solution.py:76
  8.7 196.1 %all-gather.9.cloned.1.call-start = ((), (), s32[]{:S(2)}) async-start(), calls=%async_computation.3 | async-start | bytes 5677056 | tf_op jit(solution)/shard_map/all_gather | solution.py:74
  9.4 257.8 %all-gather.11.cloned.1.call-start = ((), (), s32[]{:S(2)}) async-start(), calls=%async_computation.4 | async-start | bytes 5677056 | tf_op jit(solution)/shard_map/all_gather | solution.py:77
  10.0 376.5 %all-reduce.2.cloned.1.call-start = ((), (), s32[]{:S(2)}) async-start(), calls=%async_computation.5 | async-start | bytes 11010048 | tf_op jit(solution)/shard_map/psum | solution.py:135
  76.6 143.6 %collective-permute-start.3 = (bf16[512,256]{0,1:T(8,128)(2,1)S(1)}, bf16[512,256]{0,1:T(8,128)(2,1)S(1)}, u32[]{:S(2)}, u32[]{:S(2)}) collective-permute-start(bf16[512,256]{0,1:T(8,128)(2,1)S(1)} %maximum_bitcast_fusion.6), channel_id=1, source_target_pairs={{0,4},{4,8},{8,12},{12,16},{16,20},{20,24},{24,28},{28,32},{32,36}... | collective-permute-start | bytes 786440 | tf_op jit(solution)/shard_map/ppermute | solution.py:32
  80.5 139.8 %collective-permute-start.2 = (bf16[512,256]{0,1:T(8,128)(2,1)S(1)}, bf16[512,256]{0,1:T(8,128)(2,1)S(1)}, u32[]{:S(2)}, u32[]{:S(2)}) collective-permute-start(bf16[512,256]{0,1:T(8,128)(2,1)S(1)} %maximum_bitcast_fusion.6), channel_id=1, source_target_pairs={{0,8},{4,12},{8,16},{12,20},{16,24},{20,28},{24,32},{28,36},{32,40... | collective-permute-start | bytes 786440 | tf_op jit(solution)/shard_map/ppermute | solution.py:32
  141.0 82.1 %collective-permute-start.1 = (bf16[512,256]{1,0:T(8,128)(2,1)S(1)}, bf16[512,256]{1,0:T(8,128)(2,1)S(1)}, u32[]{:S(2)}, u32[]{:S(2)}) collective-permute-start(bf16[512,256]{1,0:T(8,128)(2,1)S(1)} %fusion.53), channel_id=1, source_target_pairs={{0,4},{4,8},{8,12},{12,16},{16,20},{20,24},{24,28},{28,32},{32,36}... | collective-permute-start | bytes 786440 | tf_op jit(solution)/shard_map/ppermute | solution.py:32
  144.9 78.3 %collective-permute-start = (bf16[512,256]{1,0:T(8,128)(2,1)S(1)}, bf16[512,256]{1,0:T(8,128)(2,1)S(1)}, u32[]{:S(2)}, u32[]{:S(2)}) collective-permute-start(bf16[512,256]{1,0:T(8,128)(2,1)S(1)} %fusion.53), channel_id=1, source_target_pairs={{0,8},{4,12},{8,16},{12,20},{16,24},{20,28},{24,32},{28,36},{32,40... | collective-permute-start | bytes 786440 | tf_op jit(solution)/shard_map/ppermute | solution.py:32
  221.7 2.7 copy-start.2
  267.2 9.5 %copy-start.3 = (f32[5376]{0:T(1024)S(1)}, f32[5376]{0:T(1024)}, u32[]{:S(2)}) copy-start(f32[5376]{0:T(1024)} %param.11) | copy-start | bytes 64516
  275.5 337.0 %reduce-scatter.4.cloned.1.call-start = ((), (), s32[]{:S(2)}) async-start(), calls=%async_computation.6 | async-start | bytes 11354112
  275.5 120.5 %collective-permute-start.4 = (bf16[512,5376]{1,0:T(8,128)(2,1)}, bf16[512,5376]{1,0:T(8,128)(2,1)}, u32[]{:S(2)}, u32[]{:S(2)}) collective-permute-start(bf16[512,5376]{1,0:T(8,128)(2,1)} %bitcast.138), channel_id=1, source_target_pairs={{0,64},{64,0},{1,65},{65,1},{2,66},{66,2},{3,67},{67,3},{4,68},{68... | collective-permute-start | bytes 16515080 | tf_op jit(solution)/shard_map/ppermute | solution.py:26
  386.5 9.5 %copy-start = (bf16[512,5376]{1,0:T(8,128)(2,1)S(1)}, bf16[512,5376]{1,0:T(8,128)(2,1)}, u32[]{:S(2)}) copy-start(bf16[512,5376]{1,0:T(8,128)(2,1)} %all-reduce.2.cloned.1.call-done) | copy-start | bytes 16515076
  403.1 8.0 %copy-start.1 = (bf16[512,5376]{1,0:T(8,128)(2,1)}, bf16[512,5376]{1,0:T(8,128)(2,1)S(1)}, u32[]{:S(2)}) copy-start(bf16[512,5376]{1,0:T(8,128)(2,1)S(1)} %get-tuple-element.13) | copy-start | bytes 16515076
  403.1 8.0 %copy-start.5 = (bf16[256,2,512]{2,0,1:T(8,128)(2,1)S(1)}, bf16[256,2,512]{2,0,1:T(8,128)(2,1)}, u32[]{:S(2)}) copy-start(bf16[256,2,512]{2,0,1:T(8,128)(2,1)} %fusion.47) | copy-start | bytes 1572868
  411.2 9.0 %slice-start.2 = ((s8[6291456]{0:T(1024)(128)(4,1)}), s8[4194304]{0:T(1024)(128)(4,1)S(1)}, s32[]{:S(2)}) async-start(s8[6291456]{0:T(1024)(128)(4,1)} %bitcast.132), calls=%async_computation.9 | async-start | bytes 8388608
  414.4 5.8 slice-start.3
  420.2 5.4 slice-start
  422.6 3.0 slice-start.1
Sparse Core Ops, SparseCore 0:
  9.7 60.2 all-gather.6
  71.7 64.1 all-gather.4
  137.7 67.0 all-gather.8
  206.4 60.7 all-gather.10
  275.6 110.8 all-reduce.1
  449.2 163.2 reduce-scatter.3
where the time goes:
time: 635 us; the launch traced here: 623 us
  waiting for transfers between devices  480 us (76%)
  matrix products  47.8 us (8%)
  other arithmetic  33.1 us (5%)
  local copies, waits for them, and re-layouts  31 us (5%)
  starting transfers between devices  16.2 us (3%)
  between operations  14.9 us (2%)
    unnamed x7, waiting for transfers between devices  162 us
    psum x1, waiting for transfers between devices, shards(): lax.psum(partial_value.astype(jnp.bfloat16), 'tensor').astype(jnp.float32)  110 us
    all_gather x1, waiting for transfers between devices, shards(): lax.all_gather(query_weight, ('sec', 'dp'), axis=0, tiled=True)  56.7 us
    all_gather x1, waiting for transfers between devices, shards(): lax.all_gather(key_weight, ('sec', 'dp'), axis=0, tiled=True)  54 us
    all_gather x1, waiting for transfers between devices, shards(): lax.all_gather(value_weight, ('sec', 'dp'), axis=0, tiled=True)  51.6 us
    all_gather x1, waiting for transfers between devices, shards(): lax.all_gather(out_weight, ('sec', 'dp'), axis=0, tiled=True)  39.8 us
    unnamed x24, local copies, waits for them, and re-layouts  18.9 us
    ppermute x4, starting transfers between devices, from_behind(): return lax.ppermute(x, axis, pairs)  14.7 us
  transfers between devices with their start and end apart: 11, of which 7 were waited for; matrix products, arithmetic and copies ran while one was open for 7% of the time, Pallas kernels for 0%

commit v1 on v0

v1 whole, which is shorter than its diff:
```python
import math

import jax
import jax.numpy as jnp
from jax import lax
from jax.experimental import pallas as pl
from jax.experimental.pallas import tpu as pltpu
from jax.sharding import PartitionSpec as P

HEADS = 8
KV_HEADS = 4
HD = 256
W = 1024
MESH = pl.DeviceIdType.MESH
VMEM_CAP = 60 * 1024 * 1024

norm_eps = 1e-06
rope_base = 10000.0
masked_score = -1e30


def where_am_i():
    sec, dp = lax.axis_index("sec"), lax.axis_index("dp")
    z = lax.div(dp, 4)
    y = lax.rem(lax.div(dp, 2), 2) * 2 + sec
    return y, z, lax.rem(dp, 2)


def mod4(v):
    return lax.rem(v + 4, 4)


def device_at(y, z, c):
    return {"sec": lax.rem(y, 2), "dp": z * 4 + lax.div(y, 2) * 2 + c}


def block_at(y, z, c):
    return lax.rem(y, 2) * 16 + z * 4 + lax.div(y, 2) * 2 + c


def greet(devices):
    barrier = pltpu.get_barrier_semaphore()
    for device in devices:
        pl.semaphore_signal(barrier, inc=1, device_id=device, device_id_type=MESH)
    pl.semaphore_wait(barrier, len(devices))


def plane_neighbours(y, z, c):
    return [
        device_at(mod4(y + 1), z, c),
        device_at(mod4(y - 1), z, c),
        device_at(y, mod4(z + 1), c),
        device_at(y, mod4(z - 1), c),
        device_at(y, z, 1 - c),
    ]


STEPS = (0, -1, 1, 2)


def gather_kernel(items, n_in, *refs):
    ins, outs = refs[:n_in], refs[n_in : 2 * n_in]
    send_sems, recv_sems, local_sems = refs[2 * n_in :]
    y, z, c = where_am_i()
    up_y, dn_y, up_z, dn_z, partner = plane_neighbours(y, z, c)
    local = []
    for k in range(n_in):
        cp = pltpu.make_async_copy(ins[k], outs[k].at[block_at(y, z, c)], local_sems.at[k])
        cp.start()
        local.append(cp)
    greet([up_y, dn_y, up_z, dn_z, partner])
    started = []

    def item_ops(i):
        k, first, cols, y_first = items[i]
        up_u, dn_u, up_v, dn_v = (up_y, dn_y, up_z, dn_z) if y_first else (up_z, dn_z, up_y, dn_y)

        def block(du, dv):
            dy, dz = (du, dv) if y_first else (dv, du)
            return block_at(mod4(y + dy), mod4(z + dz), c)

        def part(half):
            if half is None:
                return pl.ds(first, cols)
            return pl.ds(first + half * (cols // 2), cols // 2)

        def send(ev, du, dv, half, device):
            place = outs[k].at[block(du, dv), :, part(half)]
            src = ins[k].at[:, part(half)] if (du, dv) == (0, 0) else place
            cp = pltpu.make_async_remote_copy(
                src_ref=src, dst_ref=place, send_sem=send_sems.at[i, ev], recv_sem=recv_sems.at[i, ev],
                device_id=device, device_id_type=MESH,
            )
            cp.start()
            started.append(cp)

        def arrive(ev, du, dv, half, core_flip=False):
            dy, dz = (du, dv) if y_first else (dv, du)
            b = block_at(mod4(y + dy), mod4(z + dz), 1 - c if core_flip else c)
            place = outs[k].at[b, :, part(half)]
            pltpu.make_async_remote_copy(
                src_ref=place, dst_ref=place, send_sem=send_sems.at[i, ev], recv_sem=recv_sems.at[i, ev],
                device_id=partner, device_id_type=MESH,
            ).wait_recv()

        def share(du, dv):
            send(20 + STEPS.index(du) * 4 + STEPS.index(dv), du, dv, None, partner)

        def shared(du, dv):
            arrive(20 + STEPS.index(du) * 4 + STEPS.index(dv), du, dv, None, True)

        def spread(du):
            base = 4 + 4 * STEPS.index(du)
            send(base, du, 0, None, up_v)
            send(base + 1, du, 0, None, dn_v)

        def relay(du):
            base = 4 + 4 * STEPS.index(du)
            arrive(base, du, -1, None)
            send(base + 2, du, -1, 0, up_v)
            share(du, -1)
            arrive(base + 1, du, 1, None)
            send(base + 3, du, 1, 1, dn_v)
            share(du, 1)

        def far(du):
            base = 4 + 4 * STEPS.index(du)
            arrive(base + 2, du, 2, 0)
            arrive(base + 3, du, 2, 1)
            share(du, 2)

        def s0():
            send(0, 0, 0, None, up_u)
            send(1, 0, 0, None, dn_u)
            spread(0)
            share(0, 0)

        def s1():
            arrive(0, -1, 0, None)
            send(2, -1, 0, 0, up_u)
            spread(-1)
            share(-1, 0)
            arrive(1, 1, 0, None)
            send(3, 1, 0, 1, dn_u)
            spread(1)
            share(1, 0)

        def s2():
            relay(0)

        def s3():
            arrive(2, 2, 0, 0)
            arrive(3, 2, 0, 1)
            spread(2)
            share(2, 0)

        def s4():
            relay(-1)
            relay(1)

        def s5():
            far(0)

        def s6():
            relay(2)

        def s7():
            far(-1)
            far(1)
            far(2)

        def s8():
            for du in STEPS:
                for dv in STEPS:
                    shared(du, dv)

        return [s0, s1, s2, s3, s4, s5, s6, s7, s8]

    stages = [item_ops(i) for i in range(len(items))]
    for s in range(9):
        for i in range(len(items)):
            stages[i][s]()
    for cp in started:
        cp.wait_send()
    for cp in local:
        cp.wait()


def plane_gather(arrays, items, collective_id):
    n = len(arrays)

    def body(*refs):
        gather_kernel(items, n, *refs)

    size = sum(a.size for a in arrays) * 2
    return pl.pallas_call(
        body,
        out_shape=[jax.ShapeDtypeStruct((32,) + a.shape, a.dtype) for a in arrays],
        in_specs=[pl.BlockSpec(memory_space=pltpu.VMEM)] * n,
        out_specs=[pl.BlockSpec(memory_space=pl.ANY)] * n,
        scratch_shapes=[
            pltpu.SemaphoreType.DMA((len(items), 36)),
            pltpu.SemaphoreType.DMA((len(items), 36)),
            pltpu.SemaphoreType.DMA((n,)),
        ],
        compiler_params=pltpu.CompilerParams(collective_id=collective_id, has_side_effects=True),
        cost_estimate=pl.CostEstimate(flops=0, bytes_accessed=64 * size, transcendentals=0),
        name="plane_gather",
    )(*arrays)


def scatter_kernel(n_items, *refs):
    ins, outs = refs[:n_items], refs[n_items : 2 * n_items]
    other, sums, near, total, last, send_sems, recv_sems = refs[2 * n_items :]
    y, z, c = where_am_i()
    up_y, dn_y, up_z, dn_z, partner = plane_neighbours(y, z, c)
    greet([up_y, dn_y, up_z, dn_z, partner])
    cols = ins[0].shape[2]
    halves = (pl.ds(0, cols // 2), pl.ds(cols // 2, cols // 2))
    started = []

    def copy(i, ev, src, dst, device):
        return pltpu.make_async_remote_copy(
            src_ref=src, dst_ref=dst, send_sem=send_sems.at[i, ev], recv_sem=recv_sems.at[i, ev],
            device_id=device, device_id_type=MESH,
        )

    def push(i, ev, src, dst, device):
        cp = copy(i, ev, src, dst, device)
        cp.start()
        started.append(cp)

    def added(a, b):
        return a.astype(jnp.float32) + b.astype(jnp.float32)

    def axes(i):
        return (up_y, dn_y, up_z, dn_z) if i % 2 == 0 else (up_z, dn_z, up_y, dn_y)

    def place(i, du, dv, core):
        dy, dz = (du, dv) if i % 2 == 0 else (dv, du)
        return block_at(mod4(y + dy), mod4(z + dz), core)

    order = [(du, dv) for dv in (2, 1, -1, 0) for du in (2, 1, -1, 0)]

    def slot(du, dv):
        return STEPS.index(du) * 4 + STEPS.index(dv)

    for du, dv in order:
        for i in range(n_items):
            s = slot(du, dv)
            push(i, s, ins[i].at[place(i, du, dv, 1 - c)], other.at[i, s], partner)

    def combine(i, du, dv):
        s = slot(du, dv)
        copy(i, s, other.at[i, s], other.at[i, s], partner).wait_recv()
        sums[i, s] = added(ins[i][place(i, du, dv, c)], other[i, s]).astype(jnp.bfloat16)

    def ring_far(i, base, box, src, up, dn):
        push(i, base, src.at[:, halves[0]], box.at[0, :, halves[0]], up)
        push(i, base + 1, src.at[:, halves[1]], box.at[0, :, halves[1]], dn)

    def ring_near(i, base, box, plus, minus, up, dn):
        spot = box.at[0, :, halves[0]]
        copy(i, base, spot, spot, up).wait_recv()
        plus[:, halves[0]] = added(plus[:, halves[0]], box[0, :, halves[0]]).astype(jnp.bfloat16)
        push(i, base + 2, plus, box.at[1], up)
        spot = box.at[0, :, halves[1]]
        copy(i, base + 1, spot, spot, dn).wait_recv()
        minus[:, halves[1]] = added(minus[:, halves[1]], box[0, :, halves[1]]).astype(jnp.bfloat16)
        push(i, base + 3, minus, box.at[2], dn)

    def ring_end(i, base, box, own):
        copy(i, base + 2, box.at[1], box.at[1], up_y).wait_recv()
        copy(i, base + 3, box.at[2], box.at[2], up_y).wait_recv()
        return added(own[...], box[1]) + box[2].astype(jnp.float32)

    back = (2, 1, -1, 0)
    for du in back:
        for i in range(n_items):
            _, _, up_v, dn_v = axes(i)
            combine(i, du, 2)
            k = STEPS.index(du)
            ring_far(i, 16 + 4 * k, near.at[i, k], sums.at[i, slot(du, 2)], up_v, dn_v)
    for du in back:
        for i in range(n_items):
            _, _, up_v, dn_v = axes(i)
            combine(i, du, 1)
            combine(i, du, -1)
            k = STEPS.index(du)
            ring_near(i, 16 + 4 * k, near.at[i, k], sums.at[i, slot(du, 1)], sums.at[i, slot(du, -1)], up_v, dn_v)
    for du in back:
        for i in range(n_items):
            up_u, dn_u, _, _ = axes(i)
            combine(i, du, 0)
            k = STEPS.index(du)
            got = ring_end(i, 16 + 4 * k, near.at[i, k], sums.at[i, slot(du, 0)])
            total[i, k] = got.astype(jnp.bfloat16)
            if du == 2:
                ring_far(i, 32, last.at[i], total.at[i, k], up_u, dn_u)
    for i in range(n_items):
        up_u, dn_u, _, _ = axes(i)
        ring_near(i, 32, last.at[i], total.at[i, STEPS.index(1)], total.at[i, STEPS.index(-1)], up_u, dn_u)
    for i in range(n_items):
        outs[i][...] = ring_end(i, 32, last.at[i], total.at[i, 0]).astype(outs[i].dtype)
    for cp in started:
        cp.wait_send()


def plane_scatter(arrays, dtypes, collective_id):
    n = len(arrays)
    rows, cols = arrays[0].shape[1:]

    def body(*refs):
        scatter_kernel(n, *refs)

    return pl.pallas_call(
        body,
        out_shape=[jax.ShapeDtypeStruct((rows, cols), d) for d in dtypes],
        in_specs=[pl.BlockSpec(memory_space=pltpu.VMEM)] * n,
        out_specs=[pl.BlockSpec(memory_space=pltpu.VMEM)] * n,
        scratch_shapes=[
            pltpu.VMEM((n, 16, rows, cols), jnp.bfloat16),
            pltpu.VMEM((n, 16, rows, cols), jnp.bfloat16),
            pltpu.VMEM((n, 4, 3, rows, cols), jnp.bfloat16),
            pltpu.VMEM((n, 4, rows, cols), jnp.bfloat16),
            pltpu.VMEM((n, 3, rows, cols), jnp.bfloat16),
            pltpu.SemaphoreType.DMA((n, 36)),
            pltpu.SemaphoreType.DMA((n, 36)),
        ],
        compiler_params=pltpu.CompilerParams(
            collective_id=collective_id, has_side_effects=True, vmem_limit_bytes=VMEM_CAP
        ),
        name="plane_scatter",
    )(*arrays)


TILE = 128


def output_kernel(
    loss_scale, width,
    mixed, outw, student, target, gain,
    layer, pre, mixed_all, mixed_grad,
    summed, parts, boxes, stat_out, stat_in,
    send_sems, recv_sems,
):
    me = lax.axis_index("tensor")
    rows = mixed.shape[0]
    tiles = rows // TILE
    up, dn, opp = ({"tensor": mod4(me + d)} for d in (1, -1, 2))
    t_dn, t_up, t_far = mod4(me - 1), mod4(me + 1), mod4(me + 2)
    greet([up, dn, opp])
    started = []

    def copy(ev, src, dst, device):
        return pltpu.make_async_remote_copy(
            src_ref=src, dst_ref=dst, send_sem=send_sems.at[ev], recv_sem=recv_sems.at[ev],
            device_id=device, device_id_type=MESH,
        )

    def push(ev, src, dst, device):
        cp = copy(ev, src, dst, device)
        cp.start()
        started.append(cp)

    half = rows // 2
    halves = (pl.ds(0, half), pl.ds(half, half))
    push(0, mixed, mixed_all.at[me], up)
    push(1, mixed, mixed_all.at[me], dn)

    def project(t, first, source):
        @pl.loop(0, tiles)
        def _(i):
            at = pl.ds(pl.multiple_of(i * TILE, TILE), TILE)
            got = lax.dot_general(
                source[at, :], outw[t], (((1,), (1,)), ((), ())), preferred_element_type=jnp.float32
            )
            if first:
                summed[at, :] = got
            else:
                summed[at, :] += got

    project(me, True, mixed)
    mixed_all[me] = mixed[...]
    copy(0, mixed, mixed_all.at[t_dn], up).wait_recv()
    push(2, mixed_all.at[t_dn, halves[0]], mixed_all.at[t_dn, halves[0]], up)
    copy(1, mixed, mixed_all.at[t_up], dn).wait_recv()
    push(3, mixed_all.at[t_up, halves[1]], mixed_all.at[t_up, halves[1]], dn)
    project(t_dn, False, mixed_all.at[t_dn])
    project(t_up, False, mixed_all.at[t_up])
    for h in (0, 1):
        spot = mixed_all.at[t_far, halves[h]]
        copy(2 + h, spot, spot, up).wait_recv()
    project(t_far, False, mixed_all.at[t_far])

    def exchange(ev, k, fill):
        @pl.loop(0, tiles)
        def _(i):
            at = pl.ds(pl.multiple_of(i * TILE, TILE), TILE)
            column = fill(at)
            stat_out[k, :, at] = jnp.transpose(jnp.broadcast_to(column, (TILE, TILE)))[:8]

        for j, device in enumerate((up, dn, opp)):
            push(ev + j, stat_out.at[k], stat_in.at[k, j], device)
        for j, device in enumerate((up, dn, opp)):
            copy(ev + j, stat_out.at[k], stat_in.at[k, j], device).wait_recv()

    def whole_mean(k, at):
        row = stat_out[k, :, at] + stat_in[k, 0, :, at] + stat_in[k, 1, :, at] + stat_in[k, 2, :, at]
        column = jnp.transpose(jnp.broadcast_to(row[:1], (TILE, TILE)))[:, :1]
        return column * (1.0 / width)

    def squares(at):
        s = summed[at, :]
        return jnp.sum(s * s, axis=1, keepdims=True)

    exchange(4, 0, squares)

    def scaled_grad(at):
        return gain[...] * (loss_scale * (layer[at, :].astype(jnp.float32) - target[at, :].astype(jnp.float32)))

    def crossed(at):
        factor = lax.rsqrt(whole_mean(0, at) + norm_eps)
        s = summed[at, :]
        layer[at, :] = (student[at, :].astype(jnp.float32) + s * factor * gain[...]).astype(jnp.bfloat16)
        return jnp.sum(s * scaled_grad(at), axis=1, keepdims=True)

    exchange(7, 1, crossed)

    @pl.loop(0, tiles)
    def _(i):
        at = pl.ds(pl.multiple_of(i * TILE, TILE), TILE)
        factor = lax.rsqrt(whole_mean(0, at) + norm_eps)
        along = whole_mean(1, at)
        pre[at, :] = (
            factor * scaled_grad(at) - summed[at, :] * (factor * factor * factor * along)
        ).astype(jnp.bfloat16)

    def pull(t, k):
        @pl.loop(0, tiles)
        def _(i):
            at = pl.ds(pl.multiple_of(i * TILE, TILE), TILE)
            parts[k, at, :] = jnp.dot(
                pre[at, :], outw[t], preferred_element_type=jnp.float32
            ).astype(jnp.bfloat16)

    def added(a, b):
        return a.astype(jnp.float32) + b.astype(jnp.float32)

    pull(t_far, 2)
    push(10, parts.at[2, halves[0]], boxes.at[0, halves[0]], up)
    push(11, parts.at[2, halves[1]], boxes.at[0, halves[1]], dn)
    pull(t_up, 1)
    pull(t_dn, 3)
    spot = boxes.at[0, halves[0]]
    copy(10, spot, spot, up).wait_recv()
    parts[1, halves[0], :] = added(parts[1, halves[0], :], boxes[0, halves[0], :]).astype(jnp.bfloat16)
    push(12, parts.at[1], boxes.at[1], up)
    spot = boxes.at[0, halves[1]]
    copy(11, spot, spot, dn).wait_recv()
    parts[3, halves[1], :] = added(parts[3, halves[1], :], boxes[0, halves[1], :]).astype(jnp.bfloat16)
    push(13, parts.at[3], boxes.at[2], dn)
    pull(me, 0)
    copy(12, boxes.at[1], boxes.at[1], up).wait_recv()
    copy(13, boxes.at[2], boxes.at[2], dn).wait_recv()
    mixed_grad[...] = (added(parts[0], boxes[1]) + boxes[2].astype(jnp.float32)).astype(jnp.bfloat16)
    for cp in started:
        cp.wait_send()


def output_stage(mixed, outw, student, target, gain, loss_scale, width, collective_id):
    rows, cols = mixed.shape
    share = student.shape[1]

    def body(*refs):
        output_kernel(loss_scale, width, *refs)

    bf16 = jnp.bfloat16
    return pl.pallas_call(
        body,
        out_shape=[
            jax.ShapeDtypeStruct((rows, share), bf16),
            jax.ShapeDtypeStruct((rows, share), bf16),
            jax.ShapeDtypeStruct((4, rows, cols), bf16),
            jax.ShapeDtypeStruct((rows, cols), bf16),
        ],
        in_specs=[pl.BlockSpec(memory_space=pltpu.VMEM)] * 5,
        out_specs=[pl.BlockSpec(memory_space=pltpu.VMEM)] * 4,
        scratch_shapes=[
            pltpu.VMEM((rows, share), jnp.float32),
            pltpu.VMEM((4, rows, cols), bf16),
            pltpu.VMEM((3, rows, cols), bf16),
            pltpu.VMEM((2, 8, rows), jnp.float32),
            pltpu.VMEM((2, 3, 8, rows), jnp.float32),
            pltpu.SemaphoreType.DMA((14,)),
            pltpu.SemaphoreType.DMA((14,)),
        ],
        compiler_params=pltpu.CompilerParams(
            collective_id=collective_id, has_side_effects=True, vmem_limit_bytes=VMEM_CAP
        ),
        name="output_stage",
    )(mixed, outw, student, target, gain)


def from_partner(block, axis, bit):
    count = lax.axis_size(axis)
    route = []
    for low in range(count):
        high = low | 1 << bit
        if high != low and high < count:
            route += [(low, high), (high, low)]
    return lax.ppermute(block, axis, route)


def from_behind(x, axis, by):
    count = lax.axis_size(axis)
    pairs = [(i, i + by) for i in range(count) if 0 <= i + by < count]
    return lax.ppermute(x, axis, pairs)


def swap_share(block):
    route = []
    for sec in range(2):
        for dp in range(16):
            for t in range(4):
                high, low = dp // 8, dp % 8
                there = ((t // 2) * 16 + (t % 2) * 8 + low) * 4 + sec * 2 + high
                route.append(((sec * 16 + dp) * 4 + t, there))
    return lax.ppermute(block, ("sec", "dp", "tensor"), route)


def rotate(values, cos_table, sin_table, sign_value):
    row_count = values.shape[0]
    half_dim = cos_table.shape[1]
    per_head = values.reshape(row_count, -1, 2 * half_dim)
    leading = per_head[:, :, :half_dim]
    trailing = per_head[:, :, half_dim:]
    cosines = cos_table[:, None, :]
    sin_scaled = sign_value * sin_table[:, None, :]
    rotated = jnp.concatenate(
        [leading * cosines - trailing * sin_scaled, trailing * cosines + leading * sin_scaled],
        axis=2,
    )
    return rotated.reshape(row_count, -1)


def shards(
    student_rows,
    teacher_rows,
    norm_gain,
    post_gain,
    query_weight,
    key_weight,
    value_weight,
    out_weight,
):
    f32, bf16 = jnp.float32, jnp.bfloat16
    tok_count = student_rows.shape[1]
    model_width = student_rows.shape[2]
    tensor_count = lax.axis_size("tensor")
    share_cols = model_width // tensor_count
    data_count = lax.axis_size("sec") * lax.axis_size("dp")
    blocks_back = (W + tok_count - 1) // tok_count
    key_count = (blocks_back + 1) * tok_count
    local_groups = key_weight.shape[1] // HD
    group_size = HEADS // KV_HEADS
    query_cols = query_weight.shape[1]
    kv_cols = key_weight.shape[1]
    score_scale = 1.0 / math.sqrt(HD)
    loss_scale = 2.0 / math.sqrt(data_count * tok_count)
    share_start = lax.axis_index("tensor") * share_cols

    def share_of(x, axis):
        return lax.dynamic_slice_in_dim(x, share_start, share_cols, axis)

    out_block = swap_share(out_weight)
    key_value = jnp.concatenate([key_weight, value_weight], axis=1)
    items = ((0, 0, 512, True), (1, 0, 512, False), (2, 0, 256, True), (2, 256, 256, False))
    query_full, kv_full, out_share = plane_gather((query_weight, key_value, out_block), items, 0)
    query_full = query_full.reshape(model_width, query_cols)
    kv_full = kv_full.reshape(model_width, 2 * kv_cols)
    out_share = out_share.reshape(tensor_count, share_cols, query_cols)
    teacher_share, kv_full = lax.optimization_barrier((share_of(teacher_rows[0], 1), kv_full))
    target = from_partner(teacher_share, "sec", 0)

    student_f = student_rows[0].astype(f32)
    inverse = lax.rsqrt(jnp.mean(student_f * student_f, axis=1, keepdims=True) + norm_eps)
    normed = (student_f * inverse * norm_gain).astype(bf16)
    first_pos = lax.axis_index("dp") * tok_count
    half_dim = HD // 2
    inv_freq = jnp.power(f32(rope_base), -2.0 * jnp.arange(half_dim, dtype=f32) / HD)
    positions = (first_pos + jnp.arange(tok_count, dtype=jnp.int32)).astype(f32)
    angles = positions[:, None] * inv_freq[None, :]
    cos_table = jnp.cos(angles)
    sin_table = jnp.sin(angles)
    key_values = jnp.dot(normed, kv_full, preferred_element_type=f32)
    key_rows = rotate(key_values[:, :kv_cols], cos_table, sin_table, 1.0).astype(bf16)
    value_rows = key_values[:, kv_cols:].astype(bf16)
    key_parts = [key_rows]
    value_parts = [value_rows]
    for offset in range(1, blocks_back + 1):
        earlier_keys, earlier_values = from_behind((key_rows, value_rows), "dp", offset)
        key_parts = [earlier_keys] + key_parts
        value_parts = [earlier_values] + value_parts
    queries = rotate(
        jnp.dot(normed, query_full, preferred_element_type=f32), cos_table, sin_table, 1.0
    ).astype(bf16)
    key_window = jnp.concatenate(key_parts, axis=0)
    value_window = jnp.concatenate(value_parts, axis=0)
    query_pos = first_pos + jnp.arange(tok_count, dtype=jnp.int32)
    key_pos = first_pos - blocks_back * tok_count + jnp.arange(key_count, dtype=jnp.int32)
    allowed = (
        (key_pos[None, :] >= 0)
        & (key_pos[None, :] <= query_pos[:, None])
        & (key_pos[None, :] > query_pos[:, None] - W)
    )
    grouped_q = queries.reshape(tok_count, local_groups, group_size, HD)
    grouped_k = key_window.reshape(key_count, local_groups, HD)
    grouped_v = value_window.reshape(key_count, local_groups, HD)
    scores = jnp.einsum("tgad,kgd->gatk", grouped_q, grouped_k, preferred_element_type=f32) * score_scale
    scores = jnp.where(allowed, scores, masked_score)
    row_peak = jnp.max(scores, axis=3, keepdims=True)
    exp_scores = jnp.exp(scores - row_peak)
    attn_probs = exp_scores / jnp.sum(exp_scores, axis=3, keepdims=True)
    probs_b = attn_probs.astype(bf16)
    mixed_rows = (
        jnp.einsum("gatk,kgd->tgad", probs_b, grouped_v, preferred_element_type=f32)
        .astype(bf16)
        .reshape(tok_count, query_cols)
    )
    layer_share, pre_share, mixed_all, mixed_grad = output_stage(
        mixed_rows, out_share, share_of(student_rows[0], 1), target, share_of(post_gain, 0)[None],
        loss_scale, float(model_width), 1,
    )
    grouped_g = mixed_grad.reshape(tok_count, local_groups, group_size, HD)
    prob_grad = jnp.einsum("tgad,kgd->gatk", grouped_g, grouped_v, preferred_element_type=f32)
    score_grad = (
        attn_probs * (prob_grad - jnp.sum(attn_probs * prob_grad, axis=3, keepdims=True))
    ).astype(bf16)
    rotated_grad = (
        jnp.einsum("gatk,kgd->tgad", score_grad, grouped_k, preferred_element_type=f32).reshape(
            tok_count, query_cols
        )
        * score_scale
    )
    query_pre = rotate(rotated_grad, cos_table, sin_table, -1.0).astype(bf16)
    query_term = jnp.einsum("td,te->de", normed, query_pre, preferred_element_type=f32).astype(bf16)
    out_term = jnp.einsum("td,ate->ade", pre_share, mixed_all, preferred_element_type=f32).astype(bf16)
    query_grad, out_grad = plane_scatter(
        (query_term.reshape(32, -1, query_cols), out_term.reshape(32, -1, query_cols)), (f32, bf16), 2
    )
    return (layer_share[None], query_grad, swap_share(out_grad).astype(f32))


def solution(mesh):
    in_specs = (
        P("sec", "dp", None),
        P("sec", "dp", None),
        P(),
        P(),
        P(("sec", "dp"), "tensor"),
        P(("sec", "dp"), "tensor"),
        P(("sec", "dp"), "tensor"),
        P(("sec", "dp"), "tensor"),
    )
    out_specs = (P("sec", "dp", "tensor"), P(("sec", "dp"), "tensor"), P(("sec", "dp"), "tensor"))
    return jax.shard_map(shards, mesh=mesh, in_specs=in_specs, out_specs=out_specs, check_vma=False)
```

time: 635 us -> 290 us (0.46); the launches traced: 623 us -> 289 us
  waiting for transfers between devices: 480 us -> 31.3 us
  Pallas kernels: 0 us -> 156 us
  other arithmetic: 33.1 us -> 10.6 us
  between operations: 14.9 us -> 1.08 us
  starting transfers between devices: 16.2 us -> 25.3 us
  matrix products: 47.8 us -> 39.8 us
    all_gather x4 -> x0, waiting for transfers between devices: 202 us -> none  [the longest x1 56.7 us: shards(): lax.all_gather(query_weight, ('sec', 'dp'), axis=0, tiled=True)]
    unnamed x7 -> x0, waiting for transfers between devices: 162 us -> none
    pallas_call x0 -> x3, Pallas kernels: none -> 156 us  [the longest x1 54.4 us: output_stage(): pl.pallas_call(body, out_shape=[jax.ShapeDtypeStruct((rows, share), bf16)...]
    psum x1 -> x0, waiting for transfers between devices: 110 us -> none  [shards(): lax.psum(partial_value.astype(jnp.bfloat16), 'tensor').astype(jnp.float32)]
    ppermute x1, waiting for transfers between devices: 5.67 us -> 21.7 us  [from_partner(): return lax.ppermute(block, axis, route)]
    unnamed x24 -> x32, local copies, waits for them, and re-layouts: 18.9 us -> 3.97 us
    dot_general x8 -> x5, matrix products: 41.3 us -> 28.1 us  [the longest x1 6.95 us: shards(): jnp.dot(normed, query_full, preferred_element_type=f32)]
    ppermute x0 -> x2, starting transfers between devices: none -> 11.2 us  [swap_share(): return lax.ppermute(block, ('sec', 'dp', 'tensor'), route)]
  transfers between devices with their start and end apart: 11 -> 7, of which waited for: 7 -> 2; matrix products, arithmetic and copies ran while one was open for 7% -> 14% of each run, Pallas kernels for 0% -> 0%
where the time goes in v1:
time: 290 us; the launch traced here: 289 us
  Pallas kernels  156 us (54%)
  matrix products  39.8 us (14%)
  waiting for transfers between devices  31.3 us (11%)
  starting transfers between devices  25.3 us (9%)
  local copies, waits for them, and re-layouts  25 us (9%)
  other arithmetic  10.6 us (4%)
    pallas_call x1, Pallas kernels, output_stage(): pl.pallas_call(body, out_shape=[jax.ShapeDtypeStruct((rows, share), bf16)...  54.4 us
    pallas_call x1, Pallas kernels, plane_gather(): pl.pallas_call(body, out_shape=[jax.ShapeDtypeStruct((32,) + a.shape, a.d...  52.2 us
    pallas_call x1, Pallas kernels, plane_scatter(): pl.pallas_call(body, out_shape=[jax.ShapeDtypeStruct((rows, cols), d) for...  49.8 us
    ppermute x1, waiting for transfers between devices, from_partner(): return lax.ppermute(block, axis, route)  21.7 us
    ppermute x4, starting transfers between devices, from_behind(): return lax.ppermute(x, axis, pairs)  14 us
    ppermute x2, starting transfers between devices, swap_share(): return lax.ppermute(block, ('sec', 'dp', 'tensor'), route)  11.2 us
    ppermute x2, waiting for transfers between devices, swap_share(): return lax.ppermute(block, ('sec', 'dp', 'tensor'), route)  9.64 us
    dot_general x1, local copies, waits for them, and re-layouts, shards(): jnp.dot(normed, query_full, preferred_element_type=f32)  8.17 us
  transfers between devices with their start and end apart: 7, of which 2 were waited for; matrix products, arithmetic and copies ran while one was open for 14% of the time, Pallas kernels for 0%

profile of v1, /device:TPU:7, one launch (start us, length us, event | category | flops | bytes accessed | tf_op | source)
XLA Modules:
  0.0 289.5 jit_solution(7778511416548091319)
XLA Ops:
  0.6 6.4 %collective-permute-start = (bf16[168,512]{1,0:T(8,128)(2,1)}, bf16[168,512]{1,0:T(8,128)(2,1)S(1)}, u32[]{:S(2)}, u32[]{:S(2)}) collective-permute-start(bf16[168,512]{1,0:T(8,128)(2,1)} %param.15), channel_id=1, source_target_pairs={{0,0},{1,32},{2,64},{3,96},{4,4},{5,36},{6,68},{7,100},{8,8},{9,40... | collective-permute-start | bytes 516104 | tf_op jit(solution)/shard_map/ppermute | solution.py:529
  7.2 3.7 %fusion.2 = f32[512]{0:T(512)S(1)} fusion(bf16[1,512,5376]{2,1,0:T(8,128)(2,1)} %param.8), kind=kLoop, calls=%fused_computation.4 | loop fusion | flops 8257024 | bytes 5507072 | tf_op jit(solution)/shard_map/reduce_sum | solution.py:587
  10.9 3.5 %dynamic-slice_bitcast_fusion.refs_2_ = bf16[512,1344]{1,0:T(8,128)(2,1)} fusion(bf16[1,512,5376]{2,1,0:T(8,128)(2,1)} %param.8, s32[]{:T(128)S(6)} %select_n.9), kind=kLoop, calls=%fused_computation.35 | loop fusion | bytes 2752516 | tf_op jit(solution)/shard_map/dynamic_slice | solution.py:574
  14.3 2.2 constant_dynamic-slice_fusion
  23.0 52.2 %plane_gather.1 = (bf16[32,168,512]{2,1,0:T(8,128)(2,1)}, bf16[32,168,512]{2,1,0:T(8,128)(2,1)}, bf16[32,168,512]{2,1,0:T(8,128)(2,1)}) custom-call(bf16[168,512]{1,0:T(8,128)(2,1)} %refs_0_.1, bf16[168,512]{1,0:T(8,128)(2,1)} %pad_maximum_fusion.1.refs_1_, bf16[168,512]{1,0:T(8,128)(2,1)} %copy-done.5), custom_call_target="tpu_custom_call" | custom-call | bytes 33030144 | tf_op jit(solution)/shard_map/plane_gather/pallas_call | solution.py:196
  75.3 6.8 %fusion.12 = f32[512,512]{1,0:T(8,128)S(1)} fusion(bf16[5376,512]{1,0:T(8,128)(2,1)} %bitcast.143, bf16[1,512,5376]{2,1,0:T(8,128)(2,1)} %param.8, f32[5376]{0:T(1024)S(1)} %copy-done.10, f32[512]{0:T(512)S(1)} %add_rsqrt_fusion), kind=kOutput, calls=%fused_computation.19 | convolution fusion | flops 2829582336 | bytes 12082176 | tf_op jit(solution)/shard_map/dot_general | solution.py:596
  83.4 5.1 %collective-permute-start.3 = (bf16[512,256]{1,0:T(8,128)(2,1)S(1)}, bf16[512,256]{1,0:T(8,128)(2,1)}, u32[]{:S(2)}, u32[]{:S(2)}) collective-permute-start(bf16[512,256]{1,0:T(8,128)(2,1)S(1)} %maximum_bitcast_fusion.6), channel_id=1, source_target_pairs={{0,8},{4,12},{8,16},{12,20},{16,24},{20,28},{24,32},{28,36},{32,40... | collective-permute-start | bytes 786440 | tf_op jit(solution)/shard_map/ppermute | solution.py:518
  88.5 2.2 collective-permute-start.4
  91.5 4.6 %collective-permute-start.1 = (bf16[512,256]{1,0:T(8,128)(2,1)}, bf16[512,256]{1,0:T(8,128)(2,1)}, u32[]{:S(2)}, u32[]{:S(2)}) collective-permute-start(bf16[512,256]{1,0:T(8,128)(2,1)} %slice.55), channel_id=1, source_target_pairs={{0,8},{4,12},{8,16},{12,20},{16,24},{20,28},{24,32},{28,36},{32,40... | collective-permute-start | bytes 786440 | tf_op jit(solution)/shard_map/ppermute | solution.py:518
  96.0 2.1 collective-permute-start.2
  98.1 8.2 %copy.22 = bf16[512,5376]{1,0:T(8,128)(2,1)} copy(bf16[512,5376]{0,1:T(8,128)(2,1)} %bitcast.135) | data formatting | bytes 11010048 | tf_op jit(solution)/shard_map/dot_general | solution.py:606
  106.3 7.0 %fusion.14 = f32[512,2,256]{0,2,1:T(8,128)S(1)} fusion(bf16[2,256,5376]{2,1,0:T(8,128)(2,1)} %bitcast.138, bf16[1,512,5376]{2,1,0:T(8,128)(2,1)} %param.8, f32[5376]{0:T(1024)S(1)} %copy-done.10, f32[512]{0:T(512)S(1)} %add_rsqrt_fusion), kind=kOutput, calls=%fused_computation.20 | convolution fusion | flops 2829582336 | bytes 12082176 | tf_op jit(solution)/shard_map/dot_general | solution.py:606
  113.6 2.4 fusion.19
  117.5 4.0 %fusion.38 = bf16[256,2,512]{2,0,1:T(8,128)(2,1)S(1)} fusion(f32[2,512]{1,0:T(2,128)S(1)} %fusion.11, f32[2,512]{1,0:T(2,128)S(1)} %get-tuple-element.40, f32[1536,512,2]{1,0,2:T(8,128)S(1)} %get-tuple-element.41, pred[512,1536]{0,1:T(8,128)(4,1)S(1)} %compare_and_fusion, bf16[512,256]{1,0:T(8,128)(2,1)} %slice.55, ...), kind=kOutput, calls=%fused_computation.38 | convolution fusion | flops 815792128 | bytes 8396800 | tf_op jit(solution)/shard_map/gatk,kgd->tgad/dot_general | solution.py:627
  122.5 21.7 %collective-permute-done.5 = bf16[512,1344]{0,1:T(8,128)(2,1)} collective-permute-done((bf16[512,1344]{0,1:T(8,128)(2,1)S(1)}, bf16[512,1344]{0,1:T(8,128)(2,1)}, u32[]{:S(2)}, u32[]{:S(2)}) %collective-permute-start.5) | collective-permute-done | bytes 1376288 | tf_op jit(solution)/shard_map/ppermute | solution.py:512
  144.2 2.5 copy.27.refs_3_
  146.7 54.4 %output_stage.1 = (bf16[512,1344]{1,0:T(8,128)(2,1)}, bf16[512,1344]{1,0:T(8,128)(2,1)}, bf16[4,512,512]{2,1,0:T(8,128)(2,1)}, bf16[512,512]{1,0:T(8,128)(2,1)}) custom-call(bf16[512,512]{1,0:T(8,128)(2,1)} %copy.40.refs_0_, bf16[4,1344,512]{2,1,0:T(8,128)(2,1)} %bitcast.134, bf16[512,1344]{1,0:T(8,128)(2,1)} %dynamic-slice_bitcast_fusion.refs_2_, ...), custom_call_target="tpu_custom_call" | custom-call | tf_op jit(solution)/shard_map/output_stage/pallas_call | solution.py:479
  201.1 5.6 %fusion.7 = (f32[2,512]{1,0:T(2,128)S(1)}, f32[1536,512,2]{1,0,2:T(8,128)S(1)}) fusion(f32[2,512]{1,0:T(2,128)S(1)} %fusion.11, f32[2,512]{1,0:T(2,128)S(1)} %get-tuple-element.40, f32[1536,512,2]{1,0,2:T(8,128)} %copy-done, pred[512,1536]{0,1:T(8,128)(4,1)S(1)} %compare_and_fusion, bf16[64,2,8,256]{3,2,1,0:T(8,128)(2,1)} %bitcast.144, ...), kind=kOutput, calls=%fused_computation.13 | convolution fusion | flops 817101824 | bytes 14692352 | tf_op jit(solution)/shard_map/tgad,kgd->gatk/dot_general | solution.py:636
  206.8 3.8 %fusion.35 = f32[512,2,256]{0,2,1:T(8,128)S(1)} fusion(f32[1536,512,2]{1,0,2:T(8,128)S(1)} %get-tuple-element.43, f32[2,512]{1,0:T(2,128)S(1)} %get-tuple-element.42, f32[2,512]{1,0:T(2,128)S(1)} %fusion.11, f32[2,512]{1,0:T(2,128)S(1)} %get-tuple-element.40, f32[1536,512,2]{1,0,2:T(8,128)S(1)} %bitcast.133, pred[512,1536]{0,1:T(8,128)(4,1)S(1)} %compare_and_fusion, ...), kind=kOutput, calls=%fused_computation.37 | convolution fusion | flops 818937856 | bytes 15216640 | tf_op jit(solution)/shard_map/gatk,kgd->tgad/dot_general | solution.py:641
  210.9 5.4 %convolution_convert_fusion = bf16[5376,512]{1,0:T(8,128)(2,1)} fusion(bf16[512,512]{0,1:T(8,128)(2,1)S(1)} %bitcast.141, bf16[1,512,5376]{2,1,0:T(8,128)(2,1)S(1)} %bitcast.131, f32[5376]{0:T(1024)S(1)} %copy-done.10, f32[512]{0:T(512)S(1)} %add_rsqrt_fusion), kind=kOutput, calls=%fused_computation.9 | convolution fusion | flops 2832334848 | bytes 11557888 | tf_op jit(solution)/shard_map/td,te->de/dot_general | solution.py:647
  216.3 4.9 %convolution_convert_fusion.1 = bf16[4,512,1344]{1,2,0:T(8,128)(2,1)} fusion(bf16[4,512,512]{2,1,0:T(8,128)(2,1)S(1)} %copy-done.8, bf16[512,1344]{1,0:T(8,128)(2,1)S(1)} %copy-done.9), kind=kOutput, calls=%fused_computation.25 | convolution fusion | flops 2821324800 | bytes 8978432 | tf_op jit(solution)/shard_map/td,ate->ade/dot_general | solution.py:648
  221.2 49.8 %plane_scatter.1 = (f32[168,512]{1,0:T(8,128)}, bf16[168,512]{1,0:T(8,128)(2,1)}) custom-call(bf16[32,168,512]{2,1,0:T(8,128)(2,1)} %bitcast.136, bf16[32,168,512]{2,1,0:T(8,128)(2,1)} %bitcast.137), custom_call_target="tpu_custom_call" | custom-call | tf_op jit(solution)/shard_map/plane_scatter/pallas_call | solution.py:316
  271.0 4.8 %collective-permute-start.6 = (bf16[168,512]{1,0:T(8,128)(2,1)}, bf16[168,512]{1,0:T(8,128)(2,1)S(1)}, u32[]{:S(2)}, u32[]{:S(2)}) collective-permute-start(bf16[168,512]{1,0:T(8,128)(2,1)} %get-tuple-element.24), channel_id=1, source_target_pairs={{0,0},{1,32},{2,64},{3,96},{4,4},{5,36},{6,68},{7,100},{8,8},{9,40... | collective-permute-start | bytes 516104 | tf_op jit(solution)/shard_map/ppermute | solution.py:529
  277.3 9.6 %collective-permute-done.6 = bf16[168,512]{1,0:T(8,128)(2,1)S(1)} collective-permute-done((bf16[168,512]{1,0:T(8,128)(2,1)}, bf16[168,512]{1,0:T(8,128)(2,1)S(1)}, u32[]{:S(2)}, u32[]{:S(2)}) %collective-permute-start.6) | collective-permute-done | bytes 172064 | tf_op jit(solution)/shard_map/ppermute | solution.py:529
  (62 shorter events, 15.6 us)
Async XLA Ops:
  0.6 21.7 %collective-permute-start = (bf16[168,512]{1,0:T(8,128)(2,1)}, bf16[168,512]{1,0:T(8,128)(2,1)S(1)}, u32[]{:S(2)}, u32[]{:S(2)}) collective-permute-start(bf16[168,512]{1,0:T(8,128)(2,1)} %param.15), channel_id=1, source_target_pairs={{0,0},{1,32},{2,64},{3,96},{4,4},{5,36},{6,68},{7,100},{8,8},{9,40... | collective-permute-start | bytes 516104 | tf_op jit(solution)/shard_map/ppermute | solution.py:529
  10.9 8.6 %copy-start.6 = (bf16[168,256]{1,0:T(8,128)(2,1)S(1)}, bf16[168,256]{1,0:T(8,128)(2,1)}, u32[]{:S(2)}) copy-start(bf16[168,256]{1,0:T(8,128)(2,1)} %param.14) | copy-start | bytes 258052
  10.9 8.6 %copy-start.7 = (bf16[168,256]{1,0:T(8,128)(2,1)S(1)}, bf16[168,256]{1,0:T(8,128)(2,1)}, u32[]{:S(2)}) copy-start(bf16[168,256]{1,0:T(8,128)(2,1)} %param.13) | copy-start | bytes 258052
  10.9 64.4 %copy-start.10 = (f32[5376]{0:T(1024)S(1)}, f32[5376]{0:T(1024)}, u32[]{:S(2)}) copy-start(f32[5376]{0:T(1024)} %param.10) | copy-start | bytes 64516
  22.4 0.7 copy-start.5
  83.4 30.2 %copy-start.3 = (bf16[512,256]{1,0:T(8,128)(2,1)}, bf16[512,256]{1,0:T(8,128)(2,1)S(1)}, u32[]{:S(2)}) copy-start(bf16[512,256]{1,0:T(8,128)(2,1)S(1)} %maximum_bitcast_fusion.6) | copy-start | bytes 786436
  83.4 30.2 %collective-permute-start.3 = (bf16[512,256]{1,0:T(8,128)(2,1)S(1)}, bf16[512,256]{1,0:T(8,128)(2,1)}, u32[]{:S(2)}, u32[]{:S(2)}) collective-permute-start(bf16[512,256]{1,0:T(8,128)(2,1)S(1)} %maximum_bitcast_fusion.6), channel_id=1, source_target_pairs={{0,8},{4,12},{8,16},{12,20},{16,24},{20,28},{24,32},{28,36},{32,40... | collective-permute-start | bytes 786440 | tf_op jit(solution)/shard_map/ppermute | solution.py:518
  88.5 25.1 %collective-permute-start.4 = (bf16[512,256]{1,0:T(8,128)(2,1)S(1)}, bf16[512,256]{1,0:T(8,128)(2,1)}, u32[]{:S(2)}, u32[]{:S(2)}) collective-permute-start(bf16[512,256]{1,0:T(8,128)(2,1)S(1)} %maximum_bitcast_fusion.6), channel_id=1, source_target_pairs={{0,4},{4,8},{8,12},{12,16},{16,20},{20,24},{24,28},{28,32},{32,36}... | collective-permute-start | bytes 786440 | tf_op jit(solution)/shard_map/ppermute | solution.py:518
  91.5 26.0 %collective-permute-start.1 = (bf16[512,256]{1,0:T(8,128)(2,1)}, bf16[512,256]{1,0:T(8,128)(2,1)}, u32[]{:S(2)}, u32[]{:S(2)}) collective-permute-start(bf16[512,256]{1,0:T(8,128)(2,1)} %slice.55), channel_id=1, source_target_pairs={{0,8},{4,12},{8,16},{12,20},{16,24},{20,28},{24,32},{28,36},{32,40... | collective-permute-start | bytes 786440 | tf_op jit(solution)/shard_map/ppermute | solution.py:518
  96.0 21.5 %collective-permute-start.2 = (bf16[512,256]{1,0:T(8,128)(2,1)}, bf16[512,256]{1,0:T(8,128)(2,1)}, u32[]{:S(2)}, u32[]{:S(2)}) collective-permute-start(bf16[512,256]{1,0:T(8,128)(2,1)} %slice.55), channel_id=1, source_target_pairs={{0,4},{4,8},{8,12},{12,16},{16,20},{20,24},{24,28},{28,32},{32,36}... | collective-permute-start | bytes 786440 | tf_op jit(solution)/shard_map/ppermute | solution.py:518
  106.3 7.0 %copy-start.2 = (bf16[1,512,1344]{1,2,0:T(8,128)(2,1)S(1)}, bf16[1,512,1344]{1,2,0:T(8,128)(2,1)}, u32[]{:S(2)}) copy-start(bf16[1,512,1344]{1,2,0:T(8,128)(2,1)} %copy.21) | copy-start | bytes 4128772
  113.3 30.9 %collective-permute-start.5 = (bf16[512,1344]{0,1:T(8,128)(2,1)S(1)}, bf16[512,1344]{0,1:T(8,128)(2,1)}, u32[]{:S(2)}, u32[]{:S(2)}) collective-permute-start(bf16[512,1344]{0,1:T(8,128)(2,1)S(1)} %bitcast.140), channel_id=1, source_target_pairs={{0,64},{64,0},{1,65},{65,1},{2,66},{66,2},{3,67},{67,3},{4,68},{68... | collective-permute-start | bytes 4128776 | tf_op jit(solution)/shard_map/ppermute | solution.py:512
  116.0 5.5 %copy-start = (f32[1536,512,2]{1,0,2:T(8,128)}, f32[1536,512,2]{1,0,2:T(8,128)S(1)}, u32[]{:S(2)}) copy-start(f32[1536,512,2]{1,0,2:T(8,128)S(1)} %get-tuple-element.41) | copy-start | bytes 18874372
  146.7 60.0 %slice-start.2 = ((s8[6291456]{0:T(1024)(128)(4,1)}), s8[2097152]{0:T(1024)(128)(4,1)S(1)}, s32[]{:S(2)}) async-start(s8[6291456]{0:T(1024)(128)(4,1)} %bitcast.132), calls=%async_computation.2 | async-start | bytes 4194304
  201.1 5.7 %slice-start.3 = ((s8[6291456]{0:T(1024)(128)(4,1)}), s8[4194304]{0:T(1024)(128)(4,1)S(1)}, s32[]{:S(2)}) async-start(s8[6291456]{0:T(1024)(128)(4,1)} %bitcast.132), calls=%async_computation.3 | async-start | bytes 8388608
  201.1 5.7 %copy-start.4 = (bf16[512,256]{1,0:T(8,128)(2,1)S(1)}, bf16[512,256]{1,0:T(8,128)(2,1)}, u32[]{:S(2)}) copy-start(bf16[512,256]{1,0:T(8,128)(2,1)} %copy-done.3) | copy-start | bytes 786436
  201.1 9.7 %slice-start = ((s8[5505024]{0:T(1024)(128)(4,1)}), s8[4194304]{0:T(1024)(128)(4,1)S(1)}, s32[]{:S(2)}) async-start(s8[5505024]{0:T(1024)(128)(4,1)} %bitcast.130), calls=%async_computation | async-start | bytes 8388608
  206.8 4.1 %slice-start.1 = ((s8[5505024]{0:T(1024)(128)(4,1)}), s8[1310720]{0:T(1024)(128)(4,1)S(1)}, s32[]{:S(2)}) async-start(s8[5505024]{0:T(1024)(128)(4,1)} %bitcast.130), calls=%async_computation.1 | async-start | bytes 2621440
  210.9 5.4 %copy-start.8 = (bf16[4,512,512]{2,1,0:T(8,128)(2,1)S(1)}, bf16[4,512,512]{2,1,0:T(8,128)(2,1)}, u32[]{:S(2)}) copy-start(bf16[4,512,512]{2,1,0:T(8,128)(2,1)} %get-tuple-element.21) | copy-start | bytes 6291460
  210.9 5.4 %copy-start.9 = (bf16[512,1344]{1,0:T(8,128)(2,1)S(1)}, bf16[512,1344]{1,0:T(8,128)(2,1)}, u32[]{:S(2)}) copy-start(bf16[512,1344]{1,0:T(8,128)(2,1)} %get-tuple-element.22) | copy-start | bytes 4128772
  221.2 54.6 %copy-start.1 = (bf16[512,1344]{1,0:T(8,128)(2,1)S(1)}, bf16[512,1344]{1,0:T(8,128)(2,1)}, u32[]{:S(2)}) copy-start(bf16[512,1344]{1,0:T(8,128)(2,1)} %get-tuple-element.19) | copy-start | bytes 4128772
  271.0 16.0 %collective-permute-start.6 = (bf16[168,512]{1,0:T(8,128)(2,1)}, bf16[168,512]{1,0:T(8,128)(2,1)S(1)}, u32[]{:S(2)}, u32[]{:S(2)}) collective-permute-start(bf16[168,512]{1,0:T(8,128)(2,1)} %get-tuple-element.24), channel_id=1, source_target_pairs={{0,0},{1,32},{2,64},{3,96},{4,4},{5,36},{6,68},{7,100},{8,8},{9,40... | collective-permute-start | bytes 516104 | tf_op jit(solution)/shard_map/ppermute | solution.py:529
